TPU v7x, 256 devices: a whole 4x4x8 slice. The times are simulated.
256 devices in a mesh: state: 8 (over z), tile: 32 (over x, y, core).
Axes of the slice: x: 4, y: 4, z: 8, core: 2. Of those that a mesh axis runs over, the one named last changes fastest.
Arguments:
- bands: bfloat16 [8, 240, 524288], P('state', None, 'tile')
- block_slot: int32 [8, 4096], P('state', 'tile'), may hold values from 0 to 7
- tile_counties: int32 [8, 256], P('state', 'tile'), may hold values from 0 to 383, as said below
- county_place: int32 [8, 384], P('state'), may hold values from 0 to 383, as said below
- label: int32 [8, 384], P('state', 'tile'), may hold values from -200 to 200
- w_first: bfloat16 [64, 240], replicated, may hold values from -0.375 to 0.375
- taps: float32 [3, 64], replicated, may hold values from -2 to 2
- w_second: bfloat16 [128, 64], replicated, may hold values from -0.75 to 0.75
- w_third: bfloat16 [128, 128], replicated, may hold values from -0.5 to 0.5
- w_head: bfloat16 [128], replicated, may hold values from -0.5 to 0.5
Outputs:
- county_mean: float32 [8, 384], P('state', 'tile')
- weight_grads: float32 [40256], replicated
Inputs may be any that keep to these rules, and one draw needn't show every extreme that they name: `county_place`: each row is an ordering of the counties of one state region; the county at place p is owned by tile index p // 12 of that region. `tile_counties`: tile t's list names counties of its own state region owned by tile indices t, t + 1, ..., t + 4 - 1 (mod the tile axis's size); at most 4 entries of a list are owned by one tile index, and exactly 4 by t itself.
All inputs are finite; a program needn't handle non-finite values.
Results may differ from a plain program's by a relative error of at most 0.00064.
Values sent between devices are 32-bit elements; how exact they have to be, the bound alone decides.
No kernel may reach another device: no remote copies, remote signals or barrier semaphores. Data moves between devices by JAX's collectives and lax.ppermute only.
A program may use at most 128 MiB of HBM per device.

v0:
```python
import jax
import jax.numpy as jnp
from jax import lax
from jax.sharding import PartitionSpec as P

MOST = 4
REACH = 4


def from_behind(value, axis, by):
    peers = lax.axis_size(axis)
    return lax.ppermute(value, axis, [(i, (i + by) % peers) for i in range(peers)])


def silu_parts(value):
    sig = jax.nn.sigmoid(value)
    return (value * sig, sig * (1.0 + value * (1.0 - sig)))


def along_rows(field, weights, row_len):
    chans, count = field.shape
    grid = field.reshape(chans, count // row_len, row_len)
    padded = jnp.pad(grid, ((0, 0), (0, 0), (1, 1)))
    out = (
        weights[0][:, None, None] * padded[:, :, :-2]
        + weights[1][:, None, None] * grid
        + weights[2][:, None, None] * padded[:, :, 2:]
    )
    return out.reshape(chans, count)


def tap_grads(field, upstream, row_len):
    chans, count = field.shape
    grid = field.reshape(chans, count // row_len, row_len)
    padded = jnp.pad(grid, ((0, 0), (0, 0), (1, 1)))
    above = upstream.reshape(grid.shape)
    return jnp.stack(
        [
            jnp.sum(above * padded[:, :, :-2], axis=(1, 2)),
            jnp.sum(above * grid, axis=(1, 2)),
            jnp.sum(above * padded[:, :, 2:], axis=(1, 2)),
        ]
    )


def contract_last(left, right):
    return lax.dot_general(
        left, right, (((1,), (1,)), ((), ())), preferred_element_type=jnp.float32
    )


def contract_first(left, right):
    return lax.dot_general(
        left, right, (((0,), (0,)), ((), ())), preferred_element_type=jnp.float32
    )


def forward(pixels, w_first, taps, w_second, w_third, w_head, row_len):
    h_one = jnp.dot(w_first, pixels, preferred_element_type=jnp.float32)
    s_one = along_rows(h_one, taps, row_len)
    a_one = silu_parts(s_one)[0].astype(jnp.bfloat16)
    h_two = jnp.dot(w_second, a_one, preferred_element_type=jnp.float32)
    a_two = silu_parts(h_two)[0].astype(jnp.bfloat16)
    h_three = jnp.dot(w_third, a_two, preferred_element_type=jnp.float32)
    a_three = (silu_parts(h_three)[0] + a_two.astype(jnp.float32)).astype(jnp.bfloat16)
    yhat = jnp.dot(w_head, a_three, preferred_element_type=jnp.float32)
    return (h_one, s_one, a_one, h_two, a_two, h_three, a_three, yhat)


def backward(pixels, saved, taps, w_second, w_third, w_head, cotangent, row_len):
    h_one, s_one, a_one, h_two, a_two, h_three, a_three, yhat = saved
    grad_in = cotangent.astype(jnp.bfloat16)
    d_head = jnp.dot(a_three, grad_in, preferred_element_type=jnp.float32)
    d_a3 = w_head.astype(jnp.float32)[:, None] * grad_in.astype(jnp.float32)[None, :]
    d_h3 = (d_a3 * silu_parts(h_three)[1]).astype(jnp.bfloat16)
    d_third = contract_last(d_h3, a_two)
    d_a2 = contract_first(w_third, d_h3) + d_a3
    d_h2 = (d_a2 * silu_parts(h_two)[1]).astype(jnp.bfloat16)
    d_second = contract_last(d_h2, a_one)
    d_a1 = contract_first(w_second, d_h2)
    d_s1 = d_a1 * silu_parts(s_one)[1]
    d_taps = tap_grads(h_one, d_s1, row_len)
    d_h1 = along_rows(d_s1, jnp.stack([taps[2], taps[1], taps[0]]), row_len).astype(jnp.bfloat16)
    d_first = contract_last(d_h1, pixels)
    return jnp.concatenate(
        [d_first.reshape(-1), d_taps.reshape(-1), d_second.reshape(-1), d_third.reshape(-1), d_head]
    )


def slot_stats(yhat, slots, slot_count):
    blocks = slots.shape[0]
    row_len = yhat.shape[0] // blocks
    member = (slots[None, :] == jnp.arange(slot_count, dtype=jnp.int32)[:, None]).astype(
        jnp.float32
    )
    block_sums = jnp.sum(yhat.reshape(blocks, row_len), axis=1)
    return (
        jnp.sum(member * block_sums[None, :], axis=1),
        jnp.sum(member, axis=1) * row_len,
        member,
    )


def place_of(counties, table):
    hits = counties[:, None] == jnp.arange(table.shape[0], dtype=jnp.int32)[None, :]
    return jnp.sum(jnp.where(hits, table[None, :], 0), axis=1)


def judge(sums, counts, labels, devices):
    denom = jnp.maximum(counts, 1.0)
    mean = sums / denom
    live = (counts > 0.5).astype(jnp.float32)
    target = labels.astype(jnp.float32) * 0.01
    return (mean, live * 2.0 * (mean - target) / (devices * denom))


def pixel_cotangent(member, slot_adjoint, row_len):
    block_adjoint = jnp.sum(member * slot_adjoint[:, None], axis=0)
    return jnp.broadcast_to(block_adjoint[:, None], (block_adjoint.shape[0], row_len)).reshape(-1)


def settle(sums, counts, codes, labels, devices):
    flat_codes = codes.reshape(-1)
    owned = jnp.arange(1, labels.shape[0] + 1, dtype=jnp.int32).astype(jnp.float32)
    hit = (flat_codes[:, None] == owned[None, :]).astype(jnp.float32)
    total = jnp.sum(hit * sums.reshape(-1)[:, None], axis=0)
    number = jnp.sum(hit * counts.reshape(-1)[:, None], axis=0)
    mean, adjoint = judge(total, number, labels, devices)
    back = jnp.sum(hit * adjoint[None, :], axis=1).reshape(codes.shape)
    return (mean, back)


def packed(select, values, rows):
    return jnp.sum(select * values[:, None], axis=0).reshape(rows, -1)


def on_device(
    bands, block_slot, tile_counties, county_place, label, w_first, taps, w_second, w_third, w_head
):
    pixels = bands[0]
    slots = block_slot[0]
    row_len = pixels.shape[1] // slots.shape[0]
    slot_total = tile_counties.shape[1]
    saved = forward(pixels, w_first, taps, w_second, w_third, w_head, row_len)
    slot_sums, slot_counts, member = slot_stats(saved[-1], slots, slot_total)
    table = county_place[0]
    place = place_of(tile_counties[0], table)
    labels_mine = label[0]
    cty_dev = labels_mine.shape[0]
    n_tile = lax.axis_size("tile")
    devices = float(lax.axis_size("state") * n_tile)
    owner = place // cty_dev
    local_code = (place % cty_dev + 1).astype(jnp.float32)
    order = jnp.arange(slot_total, dtype=jnp.int32)
    rank = jnp.sum(
        ((owner[:, None] == owner[None, :]) & (order[None, :] < order[:, None])).astype(jnp.int32),
        axis=1,
    )
    me = lax.axis_index("tile")
    position = (owner - me) % n_tile * MOST + rank
    select = (position[:, None] == jnp.arange(REACH * MOST, dtype=jnp.int32)[None, :]).astype(
        jnp.float32
    )
    out_sums = packed(select, slot_sums, REACH)
    out_counts = packed(select, slot_counts, REACH)
    out_codes = packed(select, local_code, REACH)
    got_sums, got_counts, got_codes = ([], [], [])
    for step in range(REACH):
        if step == 0:
            piece = (out_sums[0], out_counts[0], out_codes[0])
        else:
            piece = from_behind((out_sums[step], out_counts[step], out_codes[step]), "tile", step)
        got_sums.append(piece[0])
        got_counts.append(piece[1])
        got_codes.append(piece[2])
    county_mean, back = settle(
        jnp.stack(got_sums), jnp.stack(got_counts), jnp.stack(got_codes), labels_mine, devices
    )
    rows = []
    for step in range(REACH):
        if step == 0:
            rows.append(back[0])
        else:
            rows.append(from_behind(back[step], "tile", -step))
    returned = jnp.stack(rows).reshape(-1)
    slot_adjoint = jnp.sum(select * returned[None, :], axis=1)
    cotangent = pixel_cotangent(member, slot_adjoint, row_len)
    local_grads = backward(pixels, saved, taps, w_second, w_third, w_head, cotangent, row_len)
    weight_grads = lax.psum(local_grads, ("state", "tile"))
    return (county_mean[None, :], weight_grads)


def solution(mesh):
    in_specs = (
        P("state", None, "tile"),
        P("state", "tile"),
        P("state", "tile"),
        P("state", None),
        P("state", "tile"),
        P(),
        P(),
        P(),
        P(),
        P(),
    )
    out_specs = (P("state", "tile"), P())
    return jax.shard_map(
        on_device, mesh=mesh, in_specs=in_specs, out_specs=out_specs, check_vma=False
    )
```

profile of v0, /device:TPU:1, one launch (start us, length us, event | category | flops | bytes accessed | tf_op | source)
XLA Modules:
  0.0 352.5 jit_solution(9751502985637400692)
XLA Ops:
  7.2 0.0 copy-start
  7.2 0.0 all-reduce.4.cloned.1.call-start
  7.2 0.8 slice_bitcast_fusion.5
  8.0 4.7 %fusion.5 = f32[64,128,128]{2,0,1:T(8,128)S(1)} fusion(bf16[64,240]{1,0:T(8,128)(2,1)} %param.15, bf16[1,240,16384]{2,1,0:T(8,128)(2,1)} %param.10), kind=kOutput, calls=%fused_computation.18 | convolution fusion | flops 503316480 | bytes 12089344 | tf_op jit(solution)/shard_map/dot_general | solution.py:59
  12.8 2.4 fusion.18
  15.2 4.6 %multiply_convert_fusion = (bf16[128,16384]{0,1:T(8,128)(2,1)S(1)}, f32[128,16384]{0,1:T(8,128)}) fusion(bf16[64,16384]{1,0:T(8,128)(2,1)S(1)} %fusion.18, bf16[128,64]{0,1:T(8,128)(2,1)S(1)} %copy-done.12), kind=kOutput, calls=%fused_computation.16 | convolution fusion | flops 278921216 | bytes 14696448 | tf_op jit(solution)/shard_map/dot_general | solution.py:62
  19.8 4.6 %add_convert_fusion = (bf16[128,16384]{0,1:T(8,128)(2,1)S(1)}, f32[128,16384]{0,1:T(8,128)}) fusion(bf16[128,16384]{0,1:T(8,128)(2,1)S(1)} %get-tuple-element.37, bf16[128,128]{1,0:T(8,128)(2,1)S(1)} %copy-done), kind=kOutput, calls=%fused_computation.14 | convolution fusion | flops 551550976 | bytes 16809984 | tf_op jit(solution)/shard_map/dot_general | solution.py:64
  24.5 1.9 copy-done.3
  26.5 1.2 fusion.38
  27.6 0.1 reduce_sum.147
  27.8 0.1 convert_reduce_fusion
  28.0 0.2 select_reduce_fusion
  28.2 0.2 convert_reduce_fusion.1
  28.4 0.1 select_reduce_fusion.3
  28.5 0.1 slice_bitcast_fusion.2
  28.5 2.7 collective-permute-start.3
  31.2 1.3 collective-permute-start.4
  32.5 1.7 collective-permute-start.5
  34.2 0.1 slice_bitcast_fusion.6
  34.3 0.5 collective-permute-start
  34.7 1.3 collective-permute-start.1
  36.1 0.1 slice_bitcast_fusion.1
  36.1 2.1 collective-permute-start.2
  38.3 0.5 collective-permute-start.6
  38.7 0.1 collective-permute-done.5
  38.8 0.8 collective-permute-start.7
  39.6 0.1 mul.245
  39.7 2.2 collective-permute-start.8
  41.9 0.6 collective-permute-done.2
  42.5 0.1 eq.84
  42.6 2.0 collective-permute-done.7
  44.6 1.5 collective-permute-done.8
  46.0 0.1 mul.251
  46.1 0.1 fusion.27
  46.2 0.5 fusion.40
  46.8 0.2 fusion.28
  46.9 0.1 slice_bitcast_fusion
  47.0 0.9 collective-permute-start.9
  47.9 2.0 collective-permute-start.10
  49.9 0.3 collective-permute-start.11
  50.2 0.4 collective-permute-done.10
  50.6 3.8 %collective-permute-done.11 = f32[4]{0:T(128)S(1)} collective-permute-done((f32[4]{0:T(128)S(1)}, f32[4]{0:T(128)S(1)}, u32[]{:S(2)}, u32[]{:S(2)}) %collective-permute-start.11) | collective-permute-done | bytes 48 | tf_op jit(solution)/shard_map/ppermute | solution.py:12
  54.4 0.1 mul.264
  54.5 0.2 select_reduce_fusion.2
  54.7 0.1 select_reduce_fusion.1
  54.8 0.1 broadcast_bitcast_fusion
  54.9 10.0 %fusion.4 = bf16[128,16384]{0,1:T(8,128)(2,1)S(1)} fusion(f32[128,16384]{0,1:T(8,128)} %get-tuple-element.40, f32[16384]{0:T(1024)S(1)} %get-tuple-element.18, f32[128]{0:T(128)S(1)} %convert_element_type.84), kind=kLoop, calls=%fused_computation.13 | loop fusion | flops 20971520 | bytes 12648960 | tf_op jit(solution)/shard_map/convert_element_type | solution.py:75
  64.9 1.4 convolution_bitcast_fusion.4
  66.3 0.8 slice-done.1
  67.1 7.6 %fusion.2 = bf16[128,16384]{0,1:T(8,128)(2,1)S(1)} fusion(bf16[128,16384]{0,1:T(8,128)(2,1)S(1)} %fusion.4, bf16[128,128]{1,0:T(8,128)(2,1)S(1)} %copy-done, f32[128,16384]{0,1:T(8,128)S(1)} %bitcast.178, f32[16384]{0:T(1024)S(1)} %get-tuple-element.18, f32[128]{0:T(128)S(1)} %convert_element_type.84), kind=kOutput, calls=%fused_computation.5 | convolution fusion | flops 559939584 | bytes 16876032 | tf_op jit(solution)/shard_map/dot_general | solution.py:53
  74.7 3.5 fusion.21
  78.1 2.5 multiply_reduce_fusion.2
  80.6 2.5 copy.55
  83.1 1.3 fusion.41
  84.5 0.8 copy-done.4
  85.3 0.7 convolution_bitcast_fusion.5
  86.0 0.1 reshape.183
  86.1 9.2 %fusion.8 = f32[64,240]{1,0:T(8,128)S(1)} fusion(bf16[1,240,16384]{2,1,0:T(8,128)(2,1)} %param.10, f32[64,128,128]{2,0,1:T(8,128)} %bitcast.157, f32[64]{0:T(128)S(1)} %get-tuple-element.14, f32[64]{0:T(128)S(1)} %get-tuple-element.16, f32[64]{0:T(128)S(1)} %get-tuple-element.15), kind=kOutput, calls=%fused_computation.21 | convolution fusion | flops 509607936 | bytes 12120832 | tf_op jit(solution)/shard_map/dot_general | solution.py:47
  95.3 0.1 reshape.182
  95.5 0.1 reshape.184
  95.5 0.8 concatenate.3
  96.3 0.0 all-reduce.4.cloned.1.call-update
  96.3 247.7 %all-reduce.4.cloned.1.call-done = f32[40256]{0:T(1024)} async-done(((f32[40256]{0:T(1024)}), f32[40256]{0:T(1024)}) %all-reduce.4.cloned.1.call-update) | async-done | bytes 161040 | tf_op jit(solution)/shard_map/psum | solution.py:189
  344.0 1.6 copy.57
  (45 shorter events, 0.2 us)
Async XLA Ops:
  7.2 12.7 %copy-start = (bf16[128,128]{1,0:T(8,128)(2,1)S(1)}, bf16[128,128]{1,0:T(8,128)(2,1)}, u32[]{:S(2)}) copy-start(bf16[128,128]{1,0:T(8,128)(2,1)} %param.18) | copy-start | bytes 98308
  7.2 336.8 %all-reduce.4.cloned.1.call-start = ((), (), s32[]{:S(2)}) async-start(), calls=%async_computation | async-start | bytes 327680 | tf_op jit(solution)/shard_map/psum | solution.py:189
  12.8 7.1 %copy-start.1 = (f32[64,128,128]{2,0,1:T(8,128)}, f32[64,128,128]{2,0,1:T(8,128)S(1)}, u32[]{:S(2)}) copy-start(f32[64,128,128]{2,0,1:T(8,128)S(1)} %fusion.5) | copy-start | bytes 12582916
  12.8 2.4 copy-start.12
  19.8 4.6 %copy-start.5 = (bf16[128,16384]{0,1:T(8,128)(2,1)}, bf16[128,16384]{0,1:T(8,128)(2,1)S(1)}, u32[]{:S(2)}) copy-start(bf16[128,16384]{0,1:T(8,128)(2,1)S(1)} %get-tuple-element.37) | copy-start | bytes 12582916
  19.8 6.6 %copy-start.8 = (bf16[128]{0:T(256)(128)(2,1)S(1)}, bf16[128]{0:T(256)(128)(2,1)}, u32[]{:S(2)}) copy-start(bf16[128]{0:T(256)(128)(2,1)} %param.19) | copy-start | bytes 772
  24.5 2.0 copy-start.3
  24.5 3.3 copy-start.11
  24.5 3.4 copy-start.7
  24.5 3.5 copy-start.10
  24.5 21.7 %copy-start.9 = (s32[1,12]{1,0:T(1,128)S(1)}, s32[1,12]{1,0:T(1,128)}, u32[]{:S(2)}) copy-start(s32[1,12]{1,0:T(1,128)} %param.14) | copy-start | bytes 148
  28.5 7.6 %collective-permute-start.3 = (f32[4]{0:T(128)S(1)}, f32[4]{0:T(128)S(1)}, u32[]{:S(2)}, u32[]{:S(2)}) collective-permute-start(f32[4]{0:T(128)S(1)} %get-tuple-element.26), channel_id=1, source_target_pairs={{0,1},{1,2},{2,3},{3,4},{4,5},{5,6},{6,7},{7,8},{8,9},{9,10},{10,1... | collective-permute-start | bytes 56 | tf_op jit(solution)/shard_map/ppermute | solution.py:12
  31.2 7.0 %collective-permute-start.4 = (f32[4]{0:T(128)S(1)}, f32[4]{0:T(128)S(1)}, u32[]{:S(2)}, u32[]{:S(2)}) collective-permute-start(f32[4]{0:T(128)S(1)} %get-tuple-element.25), channel_id=1, source_target_pairs={{0,2},{1,3},{2,4},{3,5},{4,6},{5,7},{6,8},{7,9},{8,10},{9,11},{10,... | collective-permute-start | bytes 56 | tf_op jit(solution)/shard_map/ppermute | solution.py:12
  32.5 6.3 %collective-permute-start.5 = (f32[4]{0:T(128)S(1)}, f32[4]{0:T(128)S(1)}, u32[]{:S(2)}, u32[]{:S(2)}) collective-permute-start(f32[4]{0:T(128)S(1)} %get-tuple-element.24), channel_id=1, source_target_pairs={{0,3},{1,4},{2,5},{3,6},{4,7},{5,8},{6,9},{7,10},{8,11},{9,12},{10... | collective-permute-start | bytes 56 | tf_op jit(solution)/shard_map/ppermute | solution.py:12
  34.3 5.4 %collective-permute-start = (f32[4]{0:T(128)S(1)}, f32[4]{0:T(128)S(1)}, u32[]{:S(2)}, u32[]{:S(2)}) collective-permute-start(f32[4]{0:T(128)S(1)} %get-tuple-element.30), channel_id=1, source_target_pairs={{0,1},{1,2},{2,3},{3,4},{4,5},{5,6},{6,7},{7,8},{8,9},{9,10},{10,1... | collective-permute-start | bytes 56 | tf_op jit(solution)/shard_map/ppermute | solution.py:12
  34.7 7.1 %collective-permute-start.1 = (f32[4]{0:T(128)S(1)}, f32[4]{0:T(128)S(1)}, u32[]{:S(2)}, u32[]{:S(2)}) collective-permute-start(f32[4]{0:T(128)S(1)} %get-tuple-element.29), channel_id=1, source_target_pairs={{0,2},{1,3},{2,4},{3,5},{4,6},{5,7},{6,8},{7,9},{8,10},{9,11},{10,... | collective-permute-start | bytes 56 | tf_op jit(solution)/shard_map/ppermute | solution.py:12
  36.1 6.3 %collective-permute-start.2 = (f32[4]{0:T(128)S(1)}, f32[4]{0:T(128)S(1)}, u32[]{:S(2)}, u32[]{:S(2)}) collective-permute-start(f32[4]{0:T(128)S(1)} %get-tuple-element.28), channel_id=1, source_target_pairs={{0,3},{1,4},{2,5},{3,6},{4,7},{5,8},{6,9},{7,10},{8,11},{9,12},{10... | collective-permute-start | bytes 56 | tf_op jit(solution)/shard_map/ppermute | solution.py:12
  38.3 4.3 %collective-permute-start.6 = (f32[4]{0:T(128)S(1)}, f32[4]{0:T(128)S(1)}, u32[]{:S(2)}, u32[]{:S(2)}) collective-permute-start(f32[4]{0:T(128)S(1)} %get-tuple-element.34), channel_id=1, source_target_pairs={{0,1},{1,2},{2,3},{3,4},{4,5},{5,6},{6,7},{7,8},{8,9},{9,10},{10,1... | collective-permute-start | bytes 56 | tf_op jit(solution)/shard_map/ppermute | solution.py:12
  38.8 5.7 %collective-permute-start.7 = (f32[4]{0:T(128)S(1)}, f32[4]{0:T(128)S(1)}, u32[]{:S(2)}, u32[]{:S(2)}) collective-permute-start(f32[4]{0:T(128)S(1)} %get-tuple-element.33), channel_id=1, source_target_pairs={{0,2},{1,3},{2,4},{3,5},{4,6},{5,7},{6,8},{7,9},{8,10},{9,11},{10,... | collective-permute-start | bytes 56 | tf_op jit(solution)/shard_map/ppermute | solution.py:12
  39.7 6.3 %collective-permute-start.8 = (f32[4]{0:T(128)S(1)}, f32[4]{0:T(128)S(1)}, u32[]{:S(2)}, u32[]{:S(2)}) collective-permute-start(f32[4]{0:T(128)S(1)} %get-tuple-element.32), channel_id=1, source_target_pairs={{0,3},{1,4},{2,5},{3,6},{4,7},{5,8},{6,9},{7,10},{8,11},{9,12},{10... | collective-permute-start | bytes 56 | tf_op jit(solution)/shard_map/ppermute | solution.py:12
  47.0 3.2 collective-permute-start.9
  47.9 2.7 collective-permute-start.10
  49.9 4.5 %collective-permute-start.11 = (f32[4]{0:T(128)S(1)}, f32[4]{0:T(128)S(1)}, u32[]{:S(2)}, u32[]{:S(2)}) collective-permute-start(f32[4]{0:T(128)S(1)} %get-tuple-element.20), channel_id=1, source_target_pairs={{0,29},{1,30},{2,31},{3,0},{4,1},{5,2},{6,3},{7,4},{8,5},{9,6},{10... | collective-permute-start | bytes 56 | tf_op jit(solution)/shard_map/ppermute | solution.py:12
  54.9 10.0 %copy-start.6 = (bf16[128,16384]{0,1:T(8,128)(2,1)S(1)}, bf16[128,16384]{0,1:T(8,128)(2,1)}, u32[]{:S(2)}) copy-start(bf16[128,16384]{0,1:T(8,128)(2,1)} %copy-done.5) | copy-start | bytes 12582916
  54.9 11.4 %slice-start = ((s8[8388608]{0:T(1024)(128)(4,1)}), s8[4194304]{0:T(1024)(128)(4,1)S(1)}, s32[]{:S(2)}) async-start(s8[8388608]{0:T(1024)(128)(4,1)} %bitcast.177), calls=%async_computation.1 | async-start | bytes 8388608
  64.9 2.2 slice-start.1
  67.1 7.6 %copy-start.2 = (f32[64,128,128]{2,0,1:T(8,128)S(1)}, f32[64,128,128]{2,0,1:T(8,128)}, u32[]{:S(2)}) copy-start(f32[64,128,128]{2,0,1:T(8,128)} %copy-done.1) | copy-start | bytes 12582916
  83.1 2.2 copy-start.4
Sparse Core Ops, SparseCore 0:
  96.5 247.5 all-reduce.3
where the time goes:
time: 353 us; the launch traced here: 352 us
  waiting for transfers between devices  256 us (73%)
  matrix products  38.8 us (11%)
  other arithmetic  16.9 us (5%)
  starting transfers between devices  16.2 us (5%)
  between operations  14.3 us (4%)
  local copies, waits for them, and re-layouts  10.2 us (3%)
    psum x1, waiting for transfers between devices, on_device(): weight_grads = lax.psum(local_grads, ('state', 'tile'))  248 us
    ppermute x12, starting transfers between devices, from_behind(): lax.ppermute(value, axis, [(i, (i + by) % peers) for i in range(peers)])  16.2 us
    dot_general x3, matrix products, contract_last(): lax.dot_general(left, right, (((1,), (1,)), ((), ())), preferred_element_...  12 us
    dot_general x2, matrix products, contract_first(): lax.dot_general(left, right, (((0,), (0,)), ((), ())), preferred_element_...  11 us
    convert_element_type x1, other arithmetic, backward(): d_h3 = (d_a3 * silu_parts(h_three)[1]).astype(jnp.bfloat16)  9.98 us
    ppermute x12, waiting for transfers between devices, from_behind(): lax.ppermute(value, axis, [(i, (i + by) % peers) for i in range(peers)])  8.37 us
  transfers between devices with their start and end apart: 13, of which 7 were waited for; matrix products, arithmetic and copies ran while one was open for 0% of the time, Pallas kernels for 0%

commit v1 on v0

--- a/solution.py
+++ b/solution.py
@@ -186,7 +186,7 @@
     slot_adjoint = jnp.sum(select * returned[None, :], axis=1)
     cotangent = pixel_cotangent(member, slot_adjoint, row_len)
     local_grads = backward(pixels, saved, taps, w_second, w_third, w_head, cotangent, row_len)
-    weight_grads = lax.psum(local_grads, ("state", "tile"))
+    weight_grads = jnp.sum(lax.all_gather(local_grads, ("state", "tile")), axis=0)
     return (county_mean[None, :], weight_grads)
 
 

time: 353 us -> 608 us (1.72)
  waiting for transfers between devices: 256 us -> 441 us
  local copies, waits for them, and re-layouts: 10.2 us -> 59.9 us
  other arithmetic: 16.9 us -> 33.7 us
    unnamed x1 -> x2, waiting for transfers between devices: 0.02 us -> 435 us
    psum x1 -> x0, waiting for transfers between devices: 248 us -> none  [on_device(): weight_grads = lax.psum(local_grads, ('state', 'tile'))]
    all_gather x0 -> x1, local copies, waits for them, and re-layouts: none -> 36.1 us  [on_device(): lax.all_gather(local_grads, ('state', 'tile'))]
    reduce_sum x0 -> x1, other arithmetic: none -> 15.5 us  [on_device(): jnp.sum(lax.all_gather(local_grads, ('state', 'tile')), axis=0)]
    unnamed x31 -> x28, local copies, waits for them, and re-layouts: 5.17 us -> 19.4 us
where the time goes in v1:
time: 608 us; the launch traced here: 606 us
  waiting for transfers between devices  441 us (73%)
  local copies, waits for them, and re-layouts  59.9 us (10%)
  matrix products  40.9 us (7%)
  other arithmetic  33.7 us (6%)
  starting transfers between devices  16.1 us (3%)
  between operations  14.3 us (2%)
    unnamed x2, waiting for transfers between devices  435 us
    all_gather x1, local copies, waits for them, and re-layouts, on_device(): lax.all_gather(local_grads, ('state', 'tile'))  36.1 us
    unnamed x28, local copies, waits for them, and re-layouts  19.4 us
    ppermute x12, starting transfers between devices, from_behind(): lax.ppermute(value, axis, [(i, (i + by) % peers) for i in range(peers)])  16.1 us
    reduce_sum x1, other arithmetic, on_device(): jnp.sum(lax.all_gather(local_grads, ('state', 'tile')), axis=0)  15.5 us
  transfers between devices with their start and end apart: 13, of which 7 were waited for; matrix products, arithmetic and copies ran while one was open for 0% of the time, Pallas kernels for 0%

profile of v1, /device:TPU:1, one launch (start us, length us, event | category | flops | bytes accessed | tf_op | source)
XLA Modules:
  0.0 606.4 jit_solution(5181082057389946123)
XLA Ops:
  7.2 0.8 slice_bitcast_fusion.5
  8.0 0.7 reduce
  8.7 0.8 select_reduce_fusion
  9.6 0.2 convert_reduce_fusion.1
  9.8 4.8 fusion.5
  14.5 2.4 fusion.18
  17.0 4.6 multiply_convert_fusion
  21.6 4.6 add_convert_fusion
  26.2 2.0 copy-done.4
  28.2 1.2 fusion.38
  29.4 0.1 reduce_sum.156
  29.5 0.1 convert_reduce_fusion
  29.7 0.1 select_reduce_fusion.3
  29.8 0.1 slice_bitcast_fusion.6
  29.8 4.3 collective-permute-start.2
  34.2 0.4 collective-permute-start.1
  34.6 0.3 collective-permute-start
  34.8 0.1 slice_bitcast_fusion.2
  34.9 2.6 collective-permute-start.5
  37.5 1.3 collective-permute-start.4
  38.9 0.5 collective-permute-start.3
  39.4 0.5 collective-permute-done.1
  39.9 0.6 collective-permute-start.8
  40.5 1.7 collective-permute-start.7
  42.2 0.1 eq.84
  42.3 0.6 collective-permute-start.6
  42.9 0.4 collective-permute-done.4
  43.3 0.1 mul.245
  43.4 2.9 collective-permute-done.8
  46.2 0.1 mul.251
  46.3 0.1 fusion.27
  46.4 0.5 fusion.40
  46.9 0.2 fusion.28
  47.1 0.1 slice_bitcast_fusion
  47.2 2.4 collective-permute-start.11
  49.6 1.2 collective-permute-start.10
  50.8 0.2 collective-permute-start.9
  51.0 0.7 collective-permute-done.11
  51.7 0.4 collective-permute-done.10
  52.1 1.7 collective-permute-done.9
  53.8 0.1 mul.264
  53.9 0.2 select_reduce_fusion.2
  54.1 0.1 select_reduce_fusion.1
  54.2 0.1 broadcast_bitcast_fusion
  54.3 10.0 %fusion.4 = bf16[128,16384]{0,1:T(8,128)(2,1)S(1)} fusion(f32[128,16384]{0,1:T(8,128)} %get-tuple-element.40, f32[16384]{0:T(1024)S(1)} %get-tuple-element.18, f32[128]{0:T(128)S(1)} %convert_element_type.84), kind=kLoop, calls=%fused_computation.13 | loop fusion | flops 20971520 | bytes 12648960 | tf_op jit(solution)/shard_map/convert_element_type | solution.py:75
  64.3 1.4 convolution_bitcast_fusion.4
  65.7 0.8 slice-done.1
  66.5 7.5 %fusion.2 = bf16[128,16384]{0,1:T(8,128)(2,1)S(1)} fusion(bf16[128,16384]{0,1:T(8,128)(2,1)S(1)} %fusion.4, bf16[128,128]{1,0:T(8,128)(2,1)S(1)} %copy-done, f32[128,16384]{0,1:T(8,128)S(1)} %bitcast.178, f32[16384]{0:T(1024)S(1)} %get-tuple-element.18, f32[128]{0:T(128)S(1)} %convert_element_type.84), kind=kOutput, calls=%fused_computation.5 | convolution fusion | flops 559939584 | bytes 16876032 | tf_op jit(solution)/shard_map/dot_general | solution.py:53
  74.0 1.3 fusion.41
  75.4 0.9 copy-done.3
  76.2 3.4 fusion.21
  79.7 2.5 multiply_reduce_fusion.2
  82.1 2.5 copy.55
  84.7 0.1 reshape.184
  84.7 9.2 %fusion.8 = f32[64,240]{1,0:T(8,128)S(1)} fusion(bf16[1,240,16384]{2,1,0:T(8,128)(2,1)} %param.10, f32[64,128,128]{2,0,1:T(8,128)} %bitcast.157, f32[64]{0:T(128)S(1)} %get-tuple-element.14, f32[64]{0:T(128)S(1)} %get-tuple-element.16, f32[64]{0:T(128)S(1)} %get-tuple-element.15), kind=kOutput, calls=%fused_computation.21 | convolution fusion | flops 509607936 | bytes 12120832 | tf_op jit(solution)/shard_map/dot_general | solution.py:47
  94.0 0.1 reshape.182
  94.1 0.1 reshape.183
  94.3 2.8 convolution_bitcast_fusion.5
  97.1 0.1 concatenate.3
  97.2 13.3 %broadcast.244 = f32[10305536]{0:T(1024)} broadcast(f32[]{:T(128)} %constant.60.clone.1), dimensions={} | broadcast | bytes 41222148
  110.5 2.5 dynamic-update-slice
  113.1 434.9 %all-reduce.5.cloned.1.call-done = f32[10305536]{0:T(1024)} async-done(((f32[10305536]{0:T(1024)}), f32[10305536]{0:T(1024)}) %all-reduce.5.cloned.1.call-update) | async-done | bytes 41222160
  548.0 36.1 %reshape.186 = f32[256,40256]{1,0:T(8,128)} reshape(f32[10305536]{0:T(1024)} %all-reduce.5.cloned.1.call-done) | data formatting | bytes 82444288 | tf_op jit(solution)/shard_map/all_gather | solution.py:189
  584.0 15.5 %reduce_sum.169 = f32[40256]{0:T(1024)} reduce(f32[256,40256]{1,0:T(8,128)} %reshape.186, f32[]{:T(128)} %constant.60.clone.1), dimensions={0}, to_apply=%region_16.17 | reduce | flops 10265280 | bytes 41383172 | tf_op jit(solution)/shard_map/reduce_sum | solution.py:189
  (44 shorter events, 0.3 us)
Async XLA Ops:
  7.2 14.4 %copy-start = (bf16[128,128]{1,0:T(8,128)(2,1)S(1)}, bf16[128,128]{1,0:T(8,128)(2,1)}, u32[]{:S(2)}) copy-start(bf16[128,128]{1,0:T(8,128)(2,1)} %param.18) | copy-start | bytes 98308
  7.2 540.8 %all-reduce.5.cloned.1.call-start = ((), (), s32[]{:S(2)}) async-start(), calls=%async_computation | async-start | bytes 82444288
  14.5 7.1 %copy-start.2 = (f32[64,128,128]{2,0,1:T(8,128)}, f32[64,128,128]{2,0,1:T(8,128)S(1)}, u32[]{:S(2)}) copy-start(f32[64,128,128]{2,0,1:T(8,128)S(1)} %fusion.5) | copy-start | bytes 12582916
  14.5 2.4 copy-start.10
  21.6 4.6 copy-start.5
  21.6 6.6 %copy-start.7 = (bf16[128]{0:T(256)(128)(2,1)S(1)}, bf16[128]{0:T(256)(128)(2,1)}, u32[]{:S(2)}) copy-start(bf16[128]{0:T(256)(128)(2,1)} %param.19) | copy-start | bytes 772
  26.2 2.0 copy-start.4
  26.2 3.3 copy-start.9
  26.2 20.2 %copy-start.8 = (s32[1,12]{1,0:T(1,128)S(1)}, s32[1,12]{1,0:T(1,128)}, u32[]{:S(2)}) copy-start(s32[1,12]{1,0:T(1,128)} %param.14) | copy-start | bytes 148
  29.8 9.1 %collective-permute-start.2 = (f32[4]{0:T(128)S(1)}, f32[4]{0:T(128)S(1)}, u32[]{:S(2)}, u32[]{:S(2)}) collective-permute-start(f32[4]{0:T(128)S(1)} %get-tuple-element.28), channel_id=1, source_target_pairs={{0,3},{1,4},{2,5},{3,6},{4,7},{5,8},{6,9},{7,10},{8,11},{9,12},{10... | collective-permute-start | bytes 56 | tf_op jit(solution)/shard_map/ppermute | solution.py:12
  34.2 5.7 collective-permute-start.1
  34.6 5.9 collective-permute-start
  34.9 7.4 %collective-permute-start.5 = (f32[4]{0:T(128)S(1)}, f32[4]{0:T(128)S(1)}, u32[]{:S(2)}, u32[]{:S(2)}) collective-permute-start(f32[4]{0:T(128)S(1)} %get-tuple-element.24), channel_id=1, source_target_pairs={{0,3},{1,4},{2,5},{3,6},{4,7},{5,8},{6,9},{7,10},{8,11},{9,12},{10... | collective-permute-start | bytes 56 | tf_op jit(solution)/shard_map/ppermute | solution.py:12
  37.5 5.7 collective-permute-start.4
  38.9 4.4 collective-permute-start.3
  39.9 6.3 %collective-permute-start.8 = (f32[4]{0:T(128)S(1)}, f32[4]{0:T(128)S(1)}, u32[]{:S(2)}, u32[]{:S(2)}) collective-permute-start(f32[4]{0:T(128)S(1)} %get-tuple-element.32), channel_id=1, source_target_pairs={{0,3},{1,4},{2,5},{3,6},{4,7},{5,8},{6,9},{7,10},{8,11},{9,12},{10... | collective-permute-start | bytes 56 | tf_op jit(solution)/shard_map/ppermute | solution.py:12
  40.5 5.7 collective-permute-start.7
  42.3 3.9 collective-permute-start.6
  47.2 4.5 collective-permute-start.11
  49.6 2.4 collective-permute-start.10
  50.8 3.0 collective-permute-start.9
  54.3 10.0 %copy-start.6 = (bf16[128,16384]{0,1:T(8,128)(2,1)S(1)}, bf16[128,16384]{0,1:T(8,128)(2,1)}, u32[]{:S(2)}) copy-start(bf16[128,16384]{0,1:T(8,128)(2,1)} %copy-done.5) | copy-start | bytes 12582916
  54.3 11.4 %slice-start = ((s8[8388608]{0:T(1024)(128)(4,1)}), s8[4194304]{0:T(1024)(128)(4,1)S(1)}, s32[]{:S(2)}) async-start(s8[8388608]{0:T(1024)(128)(4,1)} %bitcast.177), calls=%async_computation.1 | async-start | bytes 8388608
  64.3 2.2 slice-start.1
  74.0 2.2 copy-start.3
  584.0 15.5 %copy-start.1 = (bf16[128,128]{1,0:T(8,128)(2,1)S(1)}, bf16[128,128]{1,0:T(8,128)(2,1)}, u32[]{:S(2)}) copy-start(bf16[128,128]{1,0:T(8,128)(2,1)} %param.18) | copy-start | bytes 98308
Sparse Core Ops, SparseCore 0:
  113.2 434.7 all-reduce.4
